TPU v7x, 32 devices: a whole 2x2x4 slice. The times are simulated.
32 devices in a mesh: ctx: 8 (over z, y), wt: 4 (over x, core).
Axes of the slice: x: 2, y: 2, z: 4, core: 2. Of those that a mesh axis runs over, the one named last changes fastest.
Arguments:
- layer_input: bfloat16 [4, 1024, 1024], P('wt', 'ctx'), may hold values from -6 to 6
- out_grad: bfloat16 [4, 1024, 1024], P('wt', 'ctx'), may hold values from -6 to 6
- deal: int32 [8, 2], replicated, may hold values from 0 to 15, as said below
- w_qkv: bfloat16 [1024, 3072], P('wt'), may hold values from -0.1875 to 0.1875
- w_out: bfloat16 [1024, 1024], P('wt'), may hold values from -0.1875 to 0.1875
- w_up: bfloat16 [1024, 4096], P('wt'), may hold values from -0.1875 to 0.1875
- w_down: bfloat16 [4096, 1024], P('wt'), may hold values from -0.09375 to 0.09375
- norm_gain: bfloat16 [4, 1024], P(None, 'wt'), may hold values from 0.099609375 to 1.8984375
- norm_shift: bfloat16 [4, 1024], P(None, 'wt'), may hold values from -1.5 to 1.5
- bias_width: bfloat16 [4, 1024], P(None, 'wt'), may hold values from -2.5 to 2.5
- up_bias: bfloat16 [4096], P('wt'), may hold values from -2.5 to 2.5
Outputs:
- layer_out: bfloat16 [4, 1024, 1024], P('wt', 'ctx')
- input_grad: float32 [4, 1024, 1024], P('wt', 'ctx')
- grad_qkv: float32 [1024, 3072], P('wt')
- grad_out: float32 [1024, 1024], P('wt')
- grad_up: float32 [1024, 4096], P('wt')
- grad_down: float32 [4096, 1024], P('wt')
- grad_gain: float32 [4, 1024], P(None, 'wt')
- grad_shift: float32 [4, 1024], P(None, 'wt')
- grad_bias: float32 [4, 1024], P(None, 'wt')
- grad_up_bias: float32 [4096], P('wt')
Inputs may be any that keep to these rules, and one draw needn't show every extreme that they name: `deal`: pieces of 64 tokens are numbered along a sequence. Row j holds a number p below 8 and its mirror 1024 // 64 - 1 - p; every piece appears once.
All inputs are finite; a program needn't handle non-finite values.
Results may differ from a plain program's by a relative error of at most 0.015.
Values may be sent and summed in bfloat16 or wider, within the bound.
No kernel may reach another device: no remote copies, remote signals or barrier semaphores. Data moves between devices by JAX's collectives and lax.ppermute only.
A program may use at most 320 MiB of HBM per device.

v0:
```python
import math
import jax
import jax.numpy as jnp
from jax import lax
from jax.sharding import PartitionSpec as P

HEADS = 16
BLK = 256
PIECE = 64
epsilon = 1e-05
relax = 32.0


def layer_norm(value, gain, shift):
    mean = jnp.mean(value, axis=-1, keepdims=True)
    centered = value - mean
    spread = jnp.mean(centered * centered, axis=-1, keepdims=True)
    return centered * lax.rsqrt(spread + epsilon) * gain + shift


def gelu_tanh(value):
    return jax.nn.gelu(value, approximate=True)


def rows_dot(left, weight):
    return jnp.einsum("std,de->ste", left, weight, preferred_element_type=jnp.float32)


def weight_grad(left, right):
    return jnp.einsum("std,ste->de", left, right, preferred_element_type=jnp.float32)


def back_dot(grad, weight):
    return jnp.einsum("ste,de->std", grad, weight, preferred_element_type=jnp.float32)


def row_total(value):
    return jnp.sum(value.astype(jnp.float32), axis=(0, 1))


def per_device(
    layer_input,
    out_grad,
    deal,
    w_qkv,
    w_out,
    w_up,
    w_down,
    norm_gain,
    norm_shift,
    bias_width,
    up_bias,
):
    seqs, rows, width = layer_input.shape
    heads = HEADS
    head = width // heads
    prescale = 1.0 / (relax * math.sqrt(head))
    ranks = lax.axis_size("ctx")
    length = rows * ranks
    per_block = BLK // PIECE
    rank = lax.axis_index("ctx")
    chosen = jnp.arange(ranks, dtype=jnp.int32) == rank
    mine = jnp.sum(jnp.where(chosen[:, None], deal, 0), axis=0)
    query_blocks = jnp.repeat(mine, rows // 2) // per_block
    key_blocks = jnp.repeat(deal.reshape(-1), rows // 2) // per_block
    full_qkv, full_out, full_up, full_down, gains, shifts, biases, up_shift = (
        lax.all_gather(w_qkv, "wt", axis=0, tiled=True),
        lax.all_gather(w_out, "wt", axis=0, tiled=True),
        lax.all_gather(w_up, "wt", axis=0, tiled=True),
        lax.all_gather(w_down, "wt", axis=0, tiled=True),
        lax.all_gather(norm_gain, "wt", axis=1, tiled=True),
        lax.all_gather(norm_shift, "wt", axis=1, tiled=True),
        lax.all_gather(bias_width, "wt", axis=1, tiled=True),
        lax.all_gather(up_bias, "wt", axis=0, tiled=True),
    )
    gains = gains.astype(jnp.float32)
    shifts = shifts.astype(jnp.float32)
    biases = biases.astype(jnp.float32)
    up_shift = up_shift.astype(jnp.float32)
    input_float = layer_input.astype(jnp.float32)
    first = layer_norm(input_float, gains[0], shifts[0]).astype(jnp.bfloat16)
    mixed = rows_dot(first, full_qkv)
    query = (mixed[..., :width] + biases[0]).astype(jnp.bfloat16)
    kv_local = jnp.concatenate(
        [mixed[..., width : 2 * width], mixed[..., 2 * width :] + biases[1]], axis=-1
    ).astype(jnp.bfloat16)
    kv_all = lax.all_gather(kv_local, "ctx", axis=1, tiled=True)
    step = math.gcd(length, 1024)
    count = length // step
    query4 = query.reshape(seqs, rows, heads, head)

    def score_block(left, right):
        return (
            jnp.einsum("sqhd,skhd->shqk", left, right, preferred_element_type=jnp.float32)
            * prescale
        )

    def key_block(index):
        start = index * step
        piece = lax.dynamic_slice_in_dim(kv_all, start, step, 1)
        keys4 = piece[..., :width].reshape(seqs, step, heads, head)
        values4 = piece[..., width:].reshape(seqs, step, heads, head)
        visible = (
            query_blocks[:, None] >= lax.dynamic_slice_in_dim(key_blocks, start, step, 0)[None, :]
        )
        return (keys4, values4, visible)

    def probs(raw, visible, totals):
        return jnp.where(visible, jnp.exp(raw * relax - totals[..., None]), 0.0)

    def online(index, carry):
        top, total, acc = carry
        keys4, values4, visible = key_block(index)
        raw = jnp.where(visible, score_block(query4, keys4), -1e30)
        new_top = jnp.maximum(top, jnp.max(raw, axis=-1))
        terms = jnp.where(visible, jnp.exp((raw - new_top[..., None]) * relax), 0.0)
        factor = jnp.exp((top - new_top) * relax)
        total = total * factor + jnp.sum(terms, axis=-1)
        acc = acc * jnp.transpose(factor, (0, 2, 1))[..., None]
        acc = acc + jnp.einsum(
            "shqk,skhd->sqhd",
            terms.astype(jnp.bfloat16),
            values4,
            preferred_element_type=jnp.float32,
        )
        return (new_top, total, acc)

    start_top = jnp.full((seqs, heads, rows), -1e30, jnp.float32)
    start_total = jnp.zeros((seqs, heads, rows), jnp.float32)
    start_acc = jnp.zeros((seqs, rows, heads, head), jnp.float32)
    top, total, acc = lax.fori_loop(0, count, online, (start_top, start_total, start_acc))
    log_total = top * relax + jnp.log(total)
    attended_float = acc / jnp.transpose(total, (0, 2, 1))[..., None]
    attended = attended_float.reshape(seqs, rows, width).astype(jnp.bfloat16)
    branch = rows_dot(attended, full_out) + biases[2]
    resid = input_float + layer_norm(branch, gains[1], shifts[1])
    second = layer_norm(resid, gains[2], shifts[2]).astype(jnp.bfloat16)
    upper = rows_dot(second, full_up) + up_shift
    hidden = gelu_tanh(upper).astype(jnp.bfloat16)
    ffn = rows_dot(hidden, full_down) + biases[3]
    top_norm, pull_four = jax.vjp(layer_norm, ffn, gains[3], shifts[3])
    result = resid + top_norm
    d_out = out_grad.astype(jnp.float32)
    d_ffn, d_gain3, d_shift3 = pull_four(d_out)
    d_ffn = d_ffn.astype(jnp.bfloat16)
    d_bias3 = row_total(d_ffn)
    g_down = weight_grad(hidden, d_ffn)
    d_hidden = back_dot(d_ffn, full_down)
    _, pull_gelu = jax.vjp(gelu_tanh, upper)
    d_upper = pull_gelu(d_hidden)[0].astype(jnp.bfloat16)
    d_up_shift = row_total(d_upper)
    g_up = weight_grad(second, d_upper)
    d_second = back_dot(d_upper, full_up)
    _, pull_three = jax.vjp(layer_norm, resid, gains[2], shifts[2])
    d_resid_part, d_gain2, d_shift2 = pull_three(d_second)
    d_resid = d_out + d_resid_part
    _, pull_two = jax.vjp(layer_norm, branch, gains[1], shifts[1])
    d_branch, d_gain1, d_shift1 = pull_two(d_resid)
    d_branch = d_branch.astype(jnp.bfloat16)
    d_bias2 = row_total(d_branch)
    g_out = weight_grad(attended, d_branch)
    d_attended = back_dot(d_branch, full_out).astype(jnp.bfloat16)
    d_out4 = d_attended.reshape(seqs, rows, heads, head)
    delta = jnp.einsum("sqhd,sqhd->shq", d_out4.astype(jnp.float32), attended_float)

    def score_grads(q_rows, do_rows, k_rows, v_rows, visible, lse_rows, delta_rows):
        weights = probs(score_block(q_rows, k_rows), visible, lse_rows)
        d_probs = jnp.einsum("sqhd,skhd->shqk", do_rows, v_rows, preferred_element_type=jnp.float32)
        d_scores = (relax * weights * (d_probs - delta_rows[..., None])).astype(jnp.bfloat16)
        return (d_scores, weights.astype(jnp.bfloat16))

    zero_query = jnp.zeros((seqs, rows, heads, head), jnp.float32)

    def local_grads(d_query, index):
        keys4, values4, visible = key_block(index)
        d_scores, weights = score_grads(query4, d_out4, keys4, values4, visible, log_total, delta)
        d_query = (
            d_query
            + jnp.einsum("shqk,skhd->sqhd", d_scores, keys4, preferred_element_type=jnp.float32)
            * prescale
        )
        d_keys = (
            jnp.einsum("shqk,sqhd->kshd", d_scores, query4, preferred_element_type=jnp.float32)
            * prescale
        )
        d_values = jnp.einsum(
            "shqk,sqhd->kshd", weights, d_out4, preferred_element_type=jnp.float32
        )
        joined = jnp.concatenate(
            [d_keys.reshape(step, seqs, width), d_values.reshape(step, seqs, width)], axis=-1
        )
        return (d_query, joined)

    d_query, pieces = lax.scan(local_grads, zero_query, jnp.arange(count, dtype=jnp.int32))
    terms = pieces.reshape(length, seqs, 2 * width)
    d_kv = jnp.transpose(lax.psum_scatter(terms, "ctx", scatter_dimension=0, tiled=True), (1, 0, 2))
    d_query = d_query.reshape(seqs, rows, width).astype(jnp.bfloat16)
    d_kv = d_kv.astype(jnp.bfloat16)
    d_bias0 = row_total(d_query)
    d_bias1 = row_total(d_kv[..., width:])
    d_mixed = jnp.concatenate([d_query, d_kv], axis=-1)
    g_qkv = weight_grad(first, d_mixed)
    d_first = back_dot(d_mixed, full_qkv)
    _, pull_one = jax.vjp(layer_norm, input_float, gains[0], shifts[0])
    d_input_part, d_gain0, d_shift0 = pull_one(d_first)
    input_grad = d_resid + d_input_part
    grad_gain = jnp.stack([d_gain0, d_gain1, d_gain2, d_gain3])
    grad_shift = jnp.stack([d_shift0, d_shift1, d_shift2, d_shift3])
    grad_bias = jnp.stack([d_bias0, d_bias1, d_bias2, d_bias3])
    owned = (
        lax.psum_scatter(g_qkv.astype(jnp.bfloat16), "wt", scatter_dimension=0, tiled=True).astype(
            jnp.float32
        ),
        lax.psum_scatter(g_out.astype(jnp.bfloat16), "wt", scatter_dimension=0, tiled=True).astype(
            jnp.float32
        ),
        lax.psum_scatter(g_up.astype(jnp.bfloat16), "wt", scatter_dimension=0, tiled=True).astype(
            jnp.float32
        ),
        lax.psum_scatter(g_down.astype(jnp.bfloat16), "wt", scatter_dimension=0, tiled=True).astype(
            jnp.float32
        ),
        lax.psum_scatter(
            grad_gain.astype(jnp.bfloat16), "wt", scatter_dimension=1, tiled=True
        ).astype(jnp.float32),
        lax.psum_scatter(
            grad_shift.astype(jnp.bfloat16), "wt", scatter_dimension=1, tiled=True
        ).astype(jnp.float32),
        lax.psum_scatter(
            grad_bias.astype(jnp.bfloat16), "wt", scatter_dimension=1, tiled=True
        ).astype(jnp.float32),
        lax.psum_scatter(
            d_up_shift.astype(jnp.bfloat16), "wt", scatter_dimension=0, tiled=True
        ).astype(jnp.float32),
    )
    summed = lax.psum(
        (owned[0], owned[1], owned[2], owned[3], owned[4], owned[5], owned[6], owned[7]), "ctx"
    )
    return (
        result.astype(jnp.bfloat16),
        input_grad,
        summed[0],
        summed[1],
        summed[2],
        summed[3],
        summed[4],
        summed[5],
        summed[6],
        summed[7],
    )


def solution(mesh):
    in_specs = (
        P("wt", "ctx", None),
        P("wt", "ctx", None),
        P(),
        P("wt", None),
        P("wt", None),
        P("wt", None),
        P("wt", None),
        P(None, "wt"),
        P(None, "wt"),
        P(None, "wt"),
        P("wt"),
    )
    out_specs = (
        P("wt", "ctx", None),
        P("wt", "ctx", None),
        P("wt", None),
        P("wt", None),
        P("wt", None),
        P("wt", None),
        P(None, "wt"),
        P(None, "wt"),
        P(None, "wt"),
        P("wt"),
    )
    return jax.shard_map(
        per_device, mesh=mesh, in_specs=in_specs, out_specs=out_specs, check_vma=False
    )
```

profile of v0, /device:TPU:0, one launch (start us, length us, event | category | flops | bytes accessed | tf_op | source)
XLA Modules:
  0.0 1275.9 jit_solution(7949901151484038611)
XLA Ops:
  8.0 6.3 all_gather.30
  14.2 5.5 all_gather.28
  19.7 5.3 all_gather.27
  29.1 29.6 %all-gather.6.cloned.1.call-done = bf16[1024,3072]{1,0:T(8,128)(2,1)} async-done(((bf16[256,3072]{1,0:T(8,128)(2,1)}), bf16[1024,3072]{1,0:T(8,128)(2,1)}) %all-gather.6.cloned.1.call-update) | async-done | bytes 6291472 | tf_op jit(solution)/shard_map/all_gather | solution.py:67
  65.7 5.2 all_gather.34
  72.4 64.9 %all-gather.8.cloned.1.call-done = bf16[1,1024,2048]{2,1,0:T(8,128)(2,1)} async-done(((bf16[1,128,2048]{2,1,0:T(8,128)(2,1)}), bf16[1,1024,2048]{2,1,0:T(8,128)(2,1)}) %all-gather.8.cloned.1.call-update) | async-done | bytes 4194320 | tf_op jit(solution)/shard_map/all_gather | solution.py:87
  165.5 54.0 %all-gather.12.cloned.1.call-done = bf16[1024,4096]{1,0:T(8,128)(2,1)} async-done(((bf16[256,4096]{1,0:T(8,128)(2,1)}), bf16[1024,4096]{1,0:T(8,128)(2,1)}) %all-gather.12.cloned.1.call-update) | async-done | bytes 8388624 | tf_op jit(solution)/shard_map/all_gather | solution.py:69
  219.5 6.1 convolution_add_fusion
  225.6 53.7 %all-gather.14.cloned.1.call-done = bf16[4096,1024]{1,0:T(8,128)(2,1)} async-done(((bf16[1024,1024]{1,0:T(8,128)(2,1)}), bf16[4096,1024]{1,0:T(8,128)(2,1)}) %all-gather.14.cloned.1.call-update) | async-done | bytes 8388624 | tf_op jit(solution)/shard_map/all_gather | solution.py:70
  279.2 5.8 fusion.96
  307.3 5.8 multiply_convert_fusion
  322.2 7.0 convolution_convert_fusion.1
  330.2 7.2 convolution_convert_fusion
  342.6 126.1 %reduce-scatter.15.cloned.1.call-done = f32[128,1,2048]{0,2,1:T(8,128)} async-done(((f32[1024,1,2048]{0,2,1:T(8,128)}), f32[128,1,2048]{0,2,1:T(8,128)}) %reduce-scatter.15.cloned.1.call-update) | async-done | bytes 1048592 | tf_op jit(solution)/shard_map/reduce_scatter | solution.py:196
  470.1 5.1 fusion.43
  485.2 7.3 all-reduce
  492.6 10.0 reduce-scatter.19.cloned.1.call-done
  502.6 74.4 %reduce-scatter.21.cloned.1.call-done = bf16[256,4096]{1,0:T(8,128)(2,1)} async-done(((bf16[1024,4096]{1,0:T(8,128)(2,1)}), bf16[256,4096]{1,0:T(8,128)(2,1)}) %reduce-scatter.21.cloned.1.call-update) | async-done | bytes 2097168 | tf_op jit(solution)/shard_map/reduce_scatter | solution.py:217
  577.0 74.5 %reduce-scatter.23.cloned.1.call-done = bf16[1024,1024]{1,0:T(8,128)(2,1)} async-done(((bf16[4096,1024]{1,0:T(8,128)(2,1)}), bf16[1024,1024]{1,0:T(8,128)(2,1)}) %reduce-scatter.23.cloned.1.call-update) | async-done | bytes 2097168 | tf_op jit(solution)/shard_map/reduce_scatter | solution.py:220
  652.5 21.9 %reduce-scatter.25.cloned.1.call-done = bf16[256,4]{1,0:T(8,128)(2,1)} async-done(((bf16[1024,4]{1,0:T(8,128)(2,1)}), bf16[256,4]{1,0:T(8,128)(2,1)}) %reduce-scatter.25.cloned.1.call-update) | async-done | bytes 2064
  675.4 22.4 %reduce-scatter.27.cloned.1.call-done = bf16[256,4]{1,0:T(8,128)(2,1)} async-done(((bf16[1024,4]{1,0:T(8,128)(2,1)}), bf16[256,4]{1,0:T(8,128)(2,1)}) %reduce-scatter.27.cloned.1.call-update) | async-done | bytes 2064
  698.6 22.0 %reduce-scatter.29.cloned.1.call-done = bf16[256,4]{1,0:T(8,128)(2,1)} async-done(((bf16[1024,4]{1,0:T(8,128)(2,1)}), bf16[256,4]{1,0:T(8,128)(2,1)}) %reduce-scatter.29.cloned.1.call-update) | async-done | bytes 2064
  721.6 60.2 %reduce-scatter.17.cloned.1.call-done = bf16[256,3072]{1,0:T(8,128)(2,1)} async-done(((bf16[1024,3072]{1,0:T(8,128)(2,1)}), bf16[256,3072]{1,0:T(8,128)(2,1)}) %reduce-scatter.17.cloned.1.call-update) | async-done | bytes 1572880 | tf_op jit(solution)/shard_map/reduce_scatter | solution.py:211
  781.8 487.4 %all-reduce.3 = (f32[256,3072]{1,0:T(8,128)}, f32[256,1024]{1,0:T(8,128)}, f32[256,4096]{1,0:T(8,128)}, f32[1024,1024]{1,0:T(8,128)}, f32[4,256]{1,0:T(4,128)}, ...) all-reduce(bf16[256,3072]{1,0:T(8,128)(2,1)} %reduce-scatter.17.clo, ...), channel_id=1, replica_groups=mesh['ctx'=8,'wt'=4] {'ctx'}, use_global_device_ids=true, to_apply=%region_21.22 | all-reduce | flops 3149824 | bytes 18900992 | tf_op jit(solution)/shard_map/psum | solution.py:236
  (243 shorter events, 92.9 us)
Async XLA Ops:
  7.2 51.6 %all-gather.6.cloned.1.call-start = ((), (), s32[]{:S(2)}) async-start(), calls=%async_computation.8 | async-start | bytes 7864320 | tf_op jit(solution)/shard_map/all_gather | solution.py:67
  7.9 129.4 %all-gather.8.cloned.1.call-start = ((), (), s32[]{:S(2)}) async-start(), calls=%async_computation.9 | async-start | bytes 4718592 | tf_op jit(solution)/shard_map/all_gather | solution.py:87
  26.1 32.6 %copy-start.23 = (f32[128]{0:T(128)}, f32[128]{0:T(128)S(1)}, u32[]{:S(2)}) copy-start(f32[128]{0:T(128)S(1)} %broadcast_multiply_fusion.3) | copy-start | bytes 1540
  27.3 31.5 %copy-start.46 = (f32[128]{0:T(128)}, f32[128]{0:T(128)S(1)}, u32[]{:S(2)}) copy-start(f32[128]{0:T(128)S(1)} %fusion.42) | copy-start | bytes 1540
  27.3 31.4 %copy-start.25 = (f32[128]{0:T(128)}, f32[128]{0:T(128)S(1)}, u32[]{:S(2)}) copy-start(f32[128]{0:T(128)S(1)} %fusion.67) | copy-start | bytes 1540
  62.7 8.8 copy-start.44
  63.7 96.0 %all-gather.10.cloned.1.call-start = ((), (), s32[]{:S(2)}) async-start(), calls=%async_computation.10 | async-start | bytes 2621440 | tf_op jit(solution)/shard_map/all_gather | solution.py:68
  64.5 155.0 %all-gather.12.cloned.1.call-start = ((), (), s32[]{:S(2)}) async-start(), calls=%async_computation.11 | async-start | bytes 10485760 | tf_op jit(solution)/shard_map/all_gather | solution.py:69
  65.1 214.2 %all-gather.14.cloned.1.call-start = ((), (), s32[]{:S(2)}) async-start(), calls=%async_computation.12 | async-start | bytes 10485760 | tf_op jit(solution)/shard_map/all_gather | solution.py:70
  65.6 403.2 %reduce-scatter.15.cloned.1.call-start = ((), (), s32[]{:S(2)}) async-start(), calls=%async_computation.13 | async-start | bytes 9437184 | tf_op jit(solution)/shard_map/reduce_scatter | solution.py:196
  72.4 76.9 %copy-start.12 = (bf16[1,128,1024]{1,2,0:T(8,128)(2,1)}, bf16[1,128,1024]{1,2,0:T(8,128)(2,1)S(1)}, u32[]{:S(2)}) copy-start(bf16[1,128,1024]{1,2,0:T(8,128)(2,1)S(1)} %copy.36) | copy-start | bytes 786436
  154.5 8.1 copy-start.1
  279.2 8.5 slice-start.2
  279.2 6.8 copy-start.32
  279.2 8.5 slice-start.3
  319.2 183.4 %reduce-scatter.19.cloned.1.call-start = ((), (), s32[]{:S(2)}) async-start(), calls=%async_computation.15 | async-start | bytes 2621440 | tf_op jit(solution)/shard_map/reduce_scatter | solution.py:214
  322.2 254.8 %reduce-scatter.21.cloned.1.call-start = ((), (), s32[]{:S(2)}) async-start(), calls=%async_computation.16 | async-start | bytes 10485760 | tf_op jit(solution)/shard_map/reduce_scatter | solution.py:217
  329.3 322.2 %reduce-scatter.23.cloned.1.call-start = ((), (), s32[]{:S(2)}) async-start(), calls=%async_computation.17 | async-start | bytes 10485760 | tf_op jit(solution)/shard_map/reduce_scatter | solution.py:220
  337.5 337.0 %reduce-scatter.25.cloned.1.call-start = ((), (), s32[]{:S(2)}) async-start(), calls=%async_computation.18 | async-start | bytes 327680
  338.6 131.5 %copy-start.24 = (f32[128]{0:T(128)S(1)}, f32[128]{0:T(128)}, u32[]{:S(2)}) copy-start(f32[128]{0:T(128)} %copy-done.23) | copy-start | bytes 1540
  476.7 221.0 %reduce-scatter.27.cloned.1.call-start = ((), (), s32[]{:S(2)}) async-start(), calls=%async_computation.19 | async-start | bytes 327680
  477.7 243.0 %reduce-scatter.29.cloned.1.call-start = ((), (), s32[]{:S(2)}) async-start(), calls=%async_computation.20 | async-start | bytes 327680
  478.7 303.1 %reduce-scatter.17.cloned.1.call-start = ((), (), s32[]{:S(2)}) async-start(), calls=%async_computation.14 | async-start | bytes 7864320 | tf_op jit(solution)/shard_map/reduce_scatter | solution.py:211
  483.3 168.2 %copy-start.8 = (f32[1,128,1024]{2,1,0:T(8,128)S(1)}, f32[1,128,1024]{2,1,0:T(8,128)}, u32[]{:S(2)}) copy-start(f32[1,128,1024]{2,1,0:T(8,128)} %copy-done.7) | copy-start | bytes 1572868
  (46 other events, 134.0 us)
Sparse Core Ops, SparseCore 0:
  9.6 49.1 all-gather.5
  63.9 73.4 all-gather.7
  138.9 20.8 all-gather.9
  161.2 58.2 all-gather.11
  220.9 58.2 all-gather.13
  319.3 149.4 reduce-scatter.14
  472.1 30.4 reduce-scatter.18
  505.2 71.7 reduce-scatter.20
  579.7 71.7 reduce-scatter.22
  654.4 20.0 reduce-scatter.24
  677.6 20.0 reduce-scatter.26
  700.6 20.0 reduce-scatter.28
  723.4 58.3 reduce-scatter.16
where the time goes:
time: 1280 us
  waiting for transfers between devices  618 us (48%)
  blocking collectives  517 us (40%)
  matrix products  74.1 us (6%)
  local copies, waits for them, and re-layouts  28.4 us (2%)
  other arithmetic  22.6 us (2%)
  between operations  15.6 us (1%)
    psum x1, blocking collectives, per_device(): lax.psum((owned[0], owned[1], owned[2], owned[3], owned[4], owned[5], own...  487 us
    reduce_scatter x1, waiting for transfers between devices, per_device(): lax.psum_scatter(terms, 'ctx', scatter_dimension=0, tiled=True)  126 us
    reduce_scatter x1, waiting for transfers between devices, per_device(): lax.psum_scatter(g_down.astype(jnp.bfloat16), 'wt', scatter_dimension=0,...  74.5 us
    reduce_scatter x1, waiting for transfers between devices, per_device(): lax.psum_scatter(g_up.astype(jnp.bfloat16), 'wt', scatter_dimension=0, ti...  74.4 us
    unnamed x16, waiting for transfers between devices  68.9 us
    all_gather x1, waiting for transfers between devices, per_device(): kv_all = lax.all_gather(kv_local, 'ctx', axis=1, tiled=True)  64.9 us
    reduce_scatter x1, waiting for transfers between devices, per_device(): lax.psum_scatter(g_qkv.astype(jnp.bfloat16), 'wt', scatter_dimension=0, t...  60.2 us
    all_gather x1, waiting for transfers between devices, per_device(): lax.all_gather(w_up, 'wt', axis=0, tiled=True)  54 us
  transfers between devices with their start and end apart: 13, of which 13 were waited for; matrix products, arithmetic and copies ran while one was open for 6% of the time, Pallas kernels for 0%

commit v1 on v0

--- a/solution.py
+++ b/solution.py
@@ -9,6 +9,22 @@
 PIECE = 64
 epsilon = 1e-05
 relax = 32.0
+
+
+def gather_around(x, axis, dim):
+    ways, here, step = (lax.axis_size(axis), lax.axis_index(axis), x.shape[dim])
+    dims = [n * ways if d == dim else n for d, n in enumerate(x.shape)]
+    full = lax.dynamic_update_slice_in_dim(jnp.zeros(dims, x.dtype), x, here * step, axis=dim)
+    going_up = going_down = x
+    for far in range(1, ways // 2 + 1):
+        going_up = lax.ppermute(going_up, axis, [(d, (d + 1) % ways) for d in range(ways)])
+        full = lax.dynamic_update_slice_in_dim(full, going_up, (here - far) % ways * step, axis=dim)
+        if 2 * far < ways:
+            going_down = lax.ppermute(going_down, axis, [(d, (d - 1) % ways) for d in range(ways)])
+            full = lax.dynamic_update_slice_in_dim(
+                full, going_down, (here + far) % ways * step, axis=dim
+            )
+    return full
 
 
 def layer_norm(value, gain, shift):
@@ -66,7 +82,7 @@
     full_qkv, full_out, full_up, full_down, gains, shifts, biases, up_shift = (
         lax.all_gather(w_qkv, "wt", axis=0, tiled=True),
         lax.all_gather(w_out, "wt", axis=0, tiled=True),
-        lax.all_gather(w_up, "wt", axis=0, tiled=True),
+        gather_around(w_up, "wt", 0),
         lax.all_gather(w_down, "wt", axis=0, tiled=True),
         lax.all_gather(norm_gain, "wt", axis=1, tiled=True),
         lax.all_gather(norm_shift, "wt", axis=1, tiled=True),

time: 1280 us -> 1230 us (0.961)
  waiting for transfers between devices: 618 us -> 499 us
  blocking collectives: 517 us -> 559 us
  local copies, waits for them, and re-layouts: 28.4 us -> 42.1 us
    all_gather x1, waiting for transfers between devices: 64.9 us -> 0.02 us  [per_device(): kv_all = lax.all_gather(kv_local, 'ctx', axis=1, tiled=True)]
    all_gather x1 -> x0, waiting for transfers between devices: 54 us -> none  [per_device(): lax.all_gather(w_up, 'wt', axis=0, tiled=True)]
    all_gather x1, blocking collectives: 5.16 us -> 47.1 us  [per_device(): lax.all_gather(up_bias, 'wt', axis=0, tiled=True)]
    ppermute x0 -> x3, waiting for transfers between devices: none -> 13.2 us  [the longest x2 13.2 us: gather_around(): lax.ppermute(going_up, axis, [(d, (d + 1) % ways) for d in range(ways)])]
    unnamed x16 -> x15, waiting for transfers between devices: 68.9 us -> 68.4 us
  transfers between devices with their start and end apart: 13 -> 15, of which waited for: 13 -> 11; matrix products, arithmetic and copies ran while one was open for 6% -> 7% of each run, Pallas kernels for 0% -> 0%
where the time goes in v1:
time: 1230 us; the launch traced here: 1220 us
  blocking collectives  559 us (45%)
  waiting for transfers between devices  499 us (41%)
  matrix products  79.6 us (6%)
  local copies, waits for them, and re-layouts  42.1 us (3%)
  other arithmetic  22 us (2%)
  between operations  15.9 us (1%)
    psum x1, blocking collectives, per_device(): lax.psum((owned[0], owned[1], owned[2], owned[3], owned[4], owned[5], own...  487 us
    reduce_scatter x1, waiting for transfers between devices, per_device(): lax.psum_scatter(terms, 'ctx', scatter_dimension=0, tiled=True)  126 us
    reduce_scatter x1, waiting for transfers between devices, per_device(): lax.psum_scatter(g_down.astype(jnp.bfloat16), 'wt', scatter_dimension=0,...  74.6 us
    reduce_scatter x1, waiting for transfers between devices, per_device(): lax.psum_scatter(g_up.astype(jnp.bfloat16), 'wt', scatter_dimension=0, ti...  74.3 us
    unnamed x15, waiting for transfers between devices  68.4 us
    reduce_scatter x1, waiting for transfers between devices, per_device(): lax.psum_scatter(g_qkv.astype(jnp.bfloat16), 'wt', scatter_dimension=0, t...  60 us
    all_gather x1, blocking collectives, per_device(): lax.all_gather(up_bias, 'wt', axis=0, tiled=True)  47.1 us
    all_gather x1, waiting for transfers between devices, per_device(): lax.all_gather(w_down, 'wt', axis=0, tiled=True)  42.7 us
  transfers between devices with their start and end apart: 15, of which 11 were waited for; matrix products, arithmetic and copies ran while one was open for 7% of the time, Pallas kernels for 0%

profile of v1, /device:TPU:0, one launch (start us, length us, event | category | flops | bytes accessed | tf_op | source)
XLA Modules:
  0.0 1220.1 jit_solution(1808635301768154392)
XLA Ops:
  8.0 6.3 all_gather.27
  14.2 5.5 all_gather.25
  19.7 5.3 all_gather.24
  29.1 29.6 %all-gather.5.cloned.1.call-done = bf16[1024,3072]{1,0:T(8,128)(2,1)} async-done(((bf16[256,3072]{1,0:T(8,128)(2,1)}), bf16[1024,3072]{1,0:T(8,128)(2,1)}) %all-gather.5.cloned.1.call-update) | async-done | bytes 6291472 | tf_op jit(solution)/shard_map/all_gather | solution.py:83
  66.9 47.1 %all_gather.30 = bf16[4096]{0:T(1024)(128)(2,1)S(1)} all-gather(bf16[1024]{0:T(1024)(128)(2,1)S(1)} %copy-done.48), channel_id=1, replica_groups=mesh['ctx'=8,'wt'=4] {'wt'}, dimensions={0}, use_global_device_ids=true | all-gather | bytes 10240 | tf_op jit(solution)/shard_map/all_gather | solution.py:90
  127.7 13.2 %collective-permute-done.2 = bf16[256,4096]{1,0:T(8,128)(2,1)S(1)} collective-permute-done((bf16[256,4096]{1,0:T(8,128)(2,1)}, bf16[256,4096]{1,0:T(8,128)(2,1)S(1)}, u32[]{:S(2)}, u32[]{:S(2)}) %collective-permute-start.2) | collective-permute-done | bytes 2097184 | tf_op jit(solution)/shard_map/ppermute | solution.py:20
  169.2 7.6 convolution_add_fusion
  176.8 42.7 %all-gather.11.cloned.1.call-done = bf16[4096,1024]{1,0:T(8,128)(2,1)} async-done(((bf16[1024,1024]{1,0:T(8,128)(2,1)}), bf16[4096,1024]{1,0:T(8,128)(2,1)}) %all-gather.11.cloned.1.call-update) | async-done | bytes 8388624 | tf_op jit(solution)/shard_map/all_gather | solution.py:86
  219.5 5.8 fusion.96
  232.9 7.3 fusion.47
  251.4 5.8 multiply_convert_fusion
  266.3 7.0 convolution_convert_fusion.1
  274.2 7.2 convolution_convert_fusion
  286.7 126.2 %reduce-scatter.15.cloned.1.call-done = f32[128,1,2048]{0,2,1:T(8,128)} async-done(((f32[1024,1,2048]{0,2,1:T(8,128)}), f32[128,1,2048]{0,2,1:T(8,128)}) %reduce-scatter.15.cloned.1.call-update) | async-done | bytes 1048592 | tf_op jit(solution)/shard_map/reduce_scatter | solution.py:212
  414.2 5.1 fusion.43
  429.3 7.3 all-reduce
  436.7 9.9 reduce-scatter.19.cloned.1.call-done
  446.5 74.3 %reduce-scatter.21.cloned.1.call-done = bf16[256,4096]{1,0:T(8,128)(2,1)} async-done(((bf16[1024,4096]{1,0:T(8,128)(2,1)}), bf16[256,4096]{1,0:T(8,128)(2,1)}) %reduce-scatter.21.cloned.1.call-update) | async-done | bytes 2097168 | tf_op jit(solution)/shard_map/reduce_scatter | solution.py:233
  520.9 74.6 %reduce-scatter.23.cloned.1.call-done = bf16[1024,1024]{1,0:T(8,128)(2,1)} async-done(((bf16[4096,1024]{1,0:T(8,128)(2,1)}), bf16[1024,1024]{1,0:T(8,128)(2,1)}) %reduce-scatter.23.cloned.1.call-update) | async-done | bytes 2097168 | tf_op jit(solution)/shard_map/reduce_scatter | solution.py:236
  596.5 22.0 %reduce-scatter.25.cloned.1.call-done = bf16[256,4]{1,0:T(8,128)(2,1)} async-done(((bf16[1024,4]{1,0:T(8,128)(2,1)}), bf16[256,4]{1,0:T(8,128)(2,1)}) %reduce-scatter.25.cloned.1.call-update) | async-done | bytes 2064
  619.4 22.2 %reduce-scatter.27.cloned.1.call-done = bf16[256,4]{1,0:T(8,128)(2,1)} async-done(((bf16[1024,4]{1,0:T(8,128)(2,1)}), bf16[256,4]{1,0:T(8,128)(2,1)}) %reduce-scatter.27.cloned.1.call-update) | async-done | bytes 2064
  642.5 22.2 %reduce-scatter.29.cloned.1.call-done = bf16[256,4]{1,0:T(8,128)(2,1)} async-done(((bf16[1024,4]{1,0:T(8,128)(2,1)}), bf16[256,4]{1,0:T(8,128)(2,1)}) %reduce-scatter.29.cloned.1.call-update) | async-done | bytes 2064
  665.6 60.0 %reduce-scatter.17.cloned.1.call-done = bf16[256,3072]{1,0:T(8,128)(2,1)} async-done(((bf16[1024,3072]{1,0:T(8,128)(2,1)}), bf16[256,3072]{1,0:T(8,128)(2,1)}) %reduce-scatter.17.cloned.1.call-update) | async-done | bytes 1572880 | tf_op jit(solution)/shard_map/reduce_scatter | solution.py:227
  725.6 487.4 %all-reduce.3 = (f32[256,3072]{1,0:T(8,128)}, f32[256,1024]{1,0:T(8,128)}, f32[256,4096]{1,0:T(8,128)}, f32[1024,1024]{1,0:T(8,128)}, f32[4,256]{1,0:T(4,128)}, ...) all-reduce(bf16[256,3072]{1,0:T(8,128)(2,1)} %reduce-scatter.17.clo, ...), channel_id=1, replica_groups=mesh['ctx'=8,'wt'=4] {'ctx'}, use_global_device_ids=true, to_apply=%region_21.22 | all-reduce | flops 3149824 | bytes 18900992 | tf_op jit(solution)/shard_map/psum | solution.py:252
  (252 shorter events, 102.8 us)
Async XLA Ops:
  7.2 51.6 %all-gather.5.cloned.1.call-start = ((), (), s32[]{:S(2)}) async-start(), calls=%async_computation.8 | async-start | bytes 7864320 | tf_op jit(solution)/shard_map/all_gather | solution.py:83
  7.9 134.7 %all-gather.7.cloned.1.call-start = ((), (), s32[]{:S(2)}) async-start(), calls=%async_computation.9 | async-start | bytes 4718592 | tf_op jit(solution)/shard_map/all_gather | solution.py:103
  26.1 32.6 %copy-start.25 = (f32[128]{0:T(128)}, f32[128]{0:T(128)S(1)}, u32[]{:S(2)}) copy-start(f32[128]{0:T(128)S(1)} %broadcast_multiply_fusion.3) | copy-start | bytes 1540
  27.3 31.4 %copy-start.27 = (f32[128]{0:T(128)}, f32[128]{0:T(128)S(1)}, u32[]{:S(2)}) copy-start(f32[128]{0:T(128)S(1)} %fusion.67) | copy-start | bytes 1540
  62.7 51.9 %copy-start.47 = (s32[8,2]{0,1:T(2,128)S(1)}, s32[8,2]{0,1:T(2,128)}, u32[]{:S(2)}) copy-start(s32[8,2]{0,1:T(2,128)} %param.13) | copy-start | bytes 196
  63.8 100.1 %all-gather.9.cloned.1.call-start = ((), (), s32[]{:S(2)}) async-start(), calls=%async_computation.10 | async-start | bytes 2621440 | tf_op jit(solution)/shard_map/all_gather | solution.py:84
  64.5 155.0 %all-gather.11.cloned.1.call-start = ((), (), s32[]{:S(2)}) async-start(), calls=%async_computation.11 | async-start | bytes 10485760 | tf_op jit(solution)/shard_map/all_gather | solution.py:86
  65.1 347.8 %reduce-scatter.15.cloned.1.call-start = ((), (), s32[]{:S(2)}) async-start(), calls=%async_computation.12 | async-start | bytes 9437184 | tf_op jit(solution)/shard_map/reduce_scatter | solution.py:212
  65.1 50.1 %collective-permute-start = (bf16[256,4096]{1,0:T(8,128)(2,1)S(1)}, bf16[256,4096]{1,0:T(8,128)(2,1)}, u32[]{:S(2)}, u32[]{:S(2)}) collective-permute-start(bf16[256,4096]{1,0:T(8,128)(2,1)S(1)} %copy-done.14), channel_id=1, source_target_pairs={{0,1},{1,2},{2,3},{3,0},{4,5},{5,6},{6,7},{7,4},{8,9},{9,10},{10,1... | collective-permute-start | bytes 6291464 | tf_op jit(solution)/shard_map/ppermute | solution.py:20
  65.4 59.2 %collective-permute-start.1 = (bf16[256,4096]{1,0:T(8,128)(2,1)S(1)}, bf16[256,4096]{1,0:T(8,128)(2,1)}, u32[]{:S(2)}, u32[]{:S(2)}) collective-permute-start(bf16[256,4096]{1,0:T(8,128)(2,1)S(1)} %copy-done.14), channel_id=1, source_target_pairs={{0,3},{1,0},{2,1},{3,2},{4,7},{5,4},{6,5},{7,6},{8,11},{9,8},{10,9... | collective-permute-start | bytes 6291464 | tf_op jit(solution)/shard_map/ppermute | solution.py:23
  115.3 25.7 %collective-permute-start.2 = (bf16[256,4096]{1,0:T(8,128)(2,1)}, bf16[256,4096]{1,0:T(8,128)(2,1)S(1)}, u32[]{:S(2)}, u32[]{:S(2)}) collective-permute-start(bf16[256,4096]{1,0:T(8,128)(2,1)} %collective-permute-done), channel_id=1, source_target_pairs={{0,1},{1,2},{2,3},{3,0},{4,5},{5,6},{6,7},{7,4},{8,9},{9,10},{10,1... | collective-permute-start | bytes 6291464 | tf_op jit(solution)/shard_map/ppermute | solution.py:20
  142.6 12.3 %copy-start.12 = (bf16[1,128,1024]{1,2,0:T(8,128)(2,1)}, bf16[1,128,1024]{1,2,0:T(8,128)(2,1)S(1)}, u32[]{:S(2)}) copy-start(bf16[1,128,1024]{1,2,0:T(8,128)(2,1)S(1)} %copy.36) | copy-start | bytes 786436
  219.5 8.6 slice-start
  219.5 8.6 slice-start.1
  232.8 8.5 copy-start.52
  263.3 183.2 %reduce-scatter.19.cloned.1.call-start = ((), (), s32[]{:S(2)}) async-start(), calls=%async_computation.14 | async-start | bytes 2621440 | tf_op jit(solution)/shard_map/reduce_scatter | solution.py:230
  266.3 254.6 %reduce-scatter.21.cloned.1.call-start = ((), (), s32[]{:S(2)}) async-start(), calls=%async_computation.15 | async-start | bytes 10485760 | tf_op jit(solution)/shard_map/reduce_scatter | solution.py:233
  273.3 322.1 %reduce-scatter.23.cloned.1.call-start = ((), (), s32[]{:S(2)}) async-start(), calls=%async_computation.16 | async-start | bytes 10485760 | tf_op jit(solution)/shard_map/reduce_scatter | solution.py:236
  281.5 337.0 %reduce-scatter.25.cloned.1.call-start = ((), (), s32[]{:S(2)}) async-start(), calls=%async_computation.17 | async-start | bytes 327680
  282.7 131.5 %copy-start.26 = (f32[128]{0:T(128)S(1)}, f32[128]{0:T(128)}, u32[]{:S(2)}) copy-start(f32[128]{0:T(128)} %copy-done.25) | copy-start | bytes 1540
  420.8 220.8 %reduce-scatter.27.cloned.1.call-start = ((), (), s32[]{:S(2)}) async-start(), calls=%async_computation.18 | async-start | bytes 327680
  421.8 242.9 %reduce-scatter.29.cloned.1.call-start = ((), (), s32[]{:S(2)}) async-start(), calls=%async_computation.19 | async-start | bytes 327680
  422.8 302.9 %reduce-scatter.17.cloned.1.call-start = ((), (), s32[]{:S(2)}) async-start(), calls=%async_computation.13 | async-start | bytes 7864320 | tf_op jit(solution)/shard_map/reduce_scatter | solution.py:227
  427.4 168.0 %copy-start.8 = (f32[1,128,1024]{2,1,0:T(8,128)S(1)}, f32[1,128,1024]{2,1,0:T(8,128)}, u32[]{:S(2)}) copy-start(f32[1,128,1024]{2,1,0:T(8,128)} %copy-done.7) | copy-start | bytes 1572868
  (49 other events, 160.9 us)
Sparse Core Ops, SparseCore 0:
  9.6 49.1 all-gather.4
  63.9 73.3 all-gather.6
  138.9 20.8 all-gather.8
  161.2 58.2 all-gather.10
  263.4 149.4 reduce-scatter.14
  416.0 30.4 reduce-scatter.18
  449.1 71.7 reduce-scatter.20
  523.6 71.7 reduce-scatter.22
  598.5 19.9 reduce-scatter.24
  621.5 19.9 reduce-scatter.26
  644.6 20.0 reduce-scatter.28
  667.2 58.3 reduce-scatter.16
